TPU v7x, 128 devices: a whole 4x4x4 slice. The times are simulated.
128 devices in a mesh: seq: 64 (over y, x_hi, z, core), dp: 2 (over x_lo).
Axes of the slice: x: 4 (x_hi: 2, x_lo: 2; x = x_hi * 2 + x_lo), y: 4, z: 4, core: 2. Of those that a mesh axis runs over, the one named last changes fastest.
Arguments:
- acceptors: bfloat16 [2, 8192, 2560], P('dp', 'seq'), may hold values from -2 to 2
- lookups: bfloat16 [2, 8192, 2560], P('dp', 'seq'), may hold values from -0.3125 to 0.3125
- payloads: bfloat16 [2, 8192, 2560], P('dp', 'seq'), may hold values from -6 to 6
- lagged_fading_source: bfloat16 [2, 8192, 2560], P('dp', 'seq'), may hold values from -6 to 6
- response_cotangent: bfloat16 [2, 8192, 2560], P('dp', 'seq'), may hold values from -2.5 to 2.5
- fading_lowering_array: bfloat16 [2560, 128], replicated, may hold values from -0.125 to 0.125
- fading_raising_array: bfloat16 [2560, 128], replicated, may hold values from -1.25 to 1.25
- feature_fading_speed: float32 [2560], replicated, may hold values from 5.812872e-06 to 0.125
- present_reward: float32 [2560], replicated, may hold values from 2.828427 to 22.627417
Outputs:
- mixed: bfloat16 [2, 8192, 2560], P('dp', 'seq')
- grad_receptance: bfloat16 [2, 8192, 2560], P('dp', 'seq')
- lookup_deriv: bfloat16 [2, 8192, 2560], P('dp', 'seq')
- payload_deriv: bfloat16 [2, 8192, 2560], P('dp', 'seq')
- grad_decay_input: bfloat16 [2, 8192, 2560], P('dp', 'seq')
- grad_lora_a: float32 [2560, 128], P('dp')
- grad_lora_b: float32 [2560, 128], P('dp')
- grad_time_decay: float32 [2560], P('dp')
- present_reward_deriv: float32 [2560], P('dp')
All inputs are finite; a program needn't handle non-finite values.
Results may differ from a plain program's by a relative error of at most 0.006.
Values sent between devices are 32-bit elements.
A program may use at most 320 MiB of HBM per device.

v0:
```python
import jax
import jax.numpy as jnp
from jax import lax
from jax.sharding import Mesh
from jax.sharding import PartitionSpec as P

ATTENDER_TOTAL = 40
LANE_TOTAL = 64
BLOCK = 64
SEQ = ("seq_0", "seq_1", "seq_2", "seq_3")
SEQ_DP = ("seq_0", "seq_1", "seq_2", "seq_3", "dp")


HIGH = lax.Precision.HIGHEST


def filled_with(x, identity):
    return jax.tree.map(
        lambda part, zero: jnp.zeros_like(part) + jnp.asarray(zero, part.dtype), x, identity
    )


def entering_2(x, axes, combine, identity, reverse):
    before = start = filled_with(x, identity)
    subtotal = x
    for axis in reversed(axes):
        devices, mine = (lax.axis_size(axis), lax.axis_index(axis))
        pieces = jax.tree.map(lambda part: lax.all_gather(part, axis), subtotal)
        inside, subtotal = (start, start)
        for k in reversed(range(devices)) if reverse else range(devices):
            passed = k > mine if reverse else k < mine
            subtotal = combine(subtotal, jax.tree.map(lambda part: part[k], pieces))
            inside = jax.tree.map(lambda new, old: jnp.where(passed, new, old), subtotal, inside)
        before = combine(inside, before)
    return before


def contract(pattern, left, right):
    return jnp.einsum(pattern, left, right, precision=HIGH, preferred_element_type=jnp.float32)


def decay_log_values(input_rows, fading_lowering_array, fading_raising_array, feature_fading_speed):
    apply_projection = jnp.dot(
        input_rows, fading_lowering_array, preferred_element_type=jnp.float32
    )
    smoothed_values = jnp.tanh(apply_projection)
    gate_portion = smoothed_values.astype(jnp.bfloat16)
    rank_projection = lax.dot_general(
        gate_portion,
        fading_raising_array,
        (((1,), (1,)), ((), ())),
        preferred_element_type=jnp.float32,
    )
    return (
        smoothed_values,
        gate_portion,
        -feature_fading_speed[None, :] * jnp.exp(rank_projection),
    )


def compose(decays, own_states, backward):

    def advance(carry, member):
        run_decay, run_state = carry
        decay, own_state = member
        return ((run_decay * decay, decay[..., None] * run_state + own_state), carry)

    initial = (
        jnp.ones(decays.shape[1:], jnp.float32),
        jnp.zeros(own_states.shape[1:], jnp.float32),
    )
    return lax.scan(advance, initial, (decays, own_states), reverse=backward)


def follow(earlier, later):
    return (earlier[0] * later[0], later[0][..., None] * earlier[1] + later[1])


def temporal_blend_sublevel(
    acceptor_lines,
    lookups,
    payloads,
    incoming_cotangent,
    fading_exponent,
    reward_by_attender,
    adjacent_shardlink,
):
    inclusive = jnp.cumsum(fading_exponent, axis=1)
    exclusive = inclusive - fading_exponent
    middle = inclusive[:, BLOCK // 2 - 1 : BLOCK // 2]
    overall = inclusive[:, -1]
    entering = jnp.exp(exclusive)
    leaving = jnp.exp(overall[:, None] - inclusive)
    upward = jnp.exp(exclusive - middle)
    downward = jnp.exp(middle - inclusive)
    decays = jnp.exp(overall)
    reached = acceptor_lines * entering
    faded_keys = lookups * leaving
    own_states = contract("nchk,nchv->nhkv", faded_keys, payloads)
    pull_states = contract("nchk,nchv->nhkv", reached, incoming_cotangent)
    starts, block_ends = adjacent_shardlink(decays, own_states, pull_states)
    position = jnp.arange(BLOCK)
    beneath = position[:, None] > position[None, :]
    early_recept = acceptor_lines * upward
    late_keys = lookups * downward
    scores = jnp.where(beneath, contract("nthk,nshk->nhts", early_recept, late_keys), 0.0)
    present_contribution = jnp.sum(acceptor_lines * reward_by_attender * lookups, axis=-1)[
        ..., None
    ]
    blended_response = (
        contract("nhts,nshv->nthv", scores, payloads)
        + present_contribution * payloads
        + contract("nthk,nhkv->nthv", reached, starts)
    )
    grad_start = decays[..., None] * block_ends + pull_states
    products = jnp.where(beneath, contract("nthv,nshv->nhts", incoming_cotangent, payloads), 0.0)
    agreement_verify = jnp.sum(payloads * incoming_cotangent, axis=-1)[..., None]
    memory_acceptors = entering * contract(
        "nhkv,nthv->nthk", starts, incoming_cotangent
    ) + upward * contract("nhts,nshk->nthk", products, late_keys)
    memory_lookup_lines = leaving * contract(
        "nhkv,nthv->nthk", block_ends, payloads
    ) + downward * contract("nhst,nshk->nthk", products, early_recept)
    payload_deriv = (
        contract("nthk,nhkv->nthv", faded_keys, block_ends)
        + contract("nhst,nshv->nthv", scores, incoming_cotangent)
        + present_contribution * incoming_cotangent
    )
    acceptor_deriv = memory_acceptors + reward_by_attender * lookups * agreement_verify
    lookup_deriv = memory_lookup_lines + reward_by_attender * acceptor_lines * agreement_verify
    present_reward_deriv = jnp.sum(acceptor_lines * lookups * agreement_verify, axis=(0, 1))
    coupling = jnp.sum(grad_start * starts, axis=-1)
    change = lookups * memory_lookup_lines - acceptor_lines * memory_acceptors
    fading_deriv = (
        coupling[:, None] + jnp.cumsum(change, axis=1) - change - acceptor_lines * memory_acceptors
    )
    return (
        blended_response,
        acceptor_deriv,
        lookup_deriv,
        payload_deriv,
        fading_deriv,
        present_reward_deriv,
    )


def sublevel_evaluation(
    reshaped_acceptors,
    reshaped_lookups,
    reshaped_payloads,
    reshaped_source,
    incoming_cotangent_reshaped,
    fading_lowering_array,
    fading_raising_array,
    feature_fading_speed,
    present_reward,
    adjacent_shardlink,
):
    smoothed_values, gate_portion, fading_exponent = decay_log_values(
        reshaped_source, fading_lowering_array, fading_raising_array, feature_fading_speed
    )
    tokens, feature_span = reshaped_acceptors.shape
    tiling_arrangement = (tokens // BLOCK, BLOCK, ATTENDER_TOTAL, LANE_TOTAL)
    collected_outcomes = temporal_blend_sublevel(
        reshaped_acceptors.astype(jnp.float32).reshape(tiling_arrangement),
        reshaped_lookups.astype(jnp.float32).reshape(tiling_arrangement),
        reshaped_payloads.astype(jnp.float32).reshape(tiling_arrangement),
        incoming_cotangent_reshaped.astype(jnp.float32).reshape(tiling_arrangement),
        fading_exponent.reshape(tiling_arrangement),
        present_reward.reshape(ATTENDER_TOTAL, LANE_TOTAL),
        adjacent_shardlink,
    )
    (
        blended_response,
        acceptor_deriv,
        lookup_deriv,
        payload_deriv,
        fading_deriv,
        present_reward_deriv,
    ) = collected_outcomes
    slope = fading_deriv.reshape(tokens, feature_span) * fading_exponent
    slope_portion = slope.astype(jnp.bfloat16)
    gate_gradient = jnp.dot(slope_portion, fading_raising_array, preferred_element_type=jnp.float32)
    projection_gradient = (gate_gradient * (1.0 - smoothed_values * smoothed_values)).astype(
        jnp.bfloat16
    )
    input_gradient = lax.dot_general(
        projection_gradient,
        fading_lowering_array,
        (((1,), (1,)), ((), ())),
        preferred_element_type=jnp.float32,
    ).astype(jnp.bfloat16)
    lowering_array_deriv = lax.dot_general(
        reshaped_source,
        projection_gradient,
        (((0,), (0,)), ((), ())),
        preferred_element_type=jnp.float32,
    )
    raising_array_deriv = lax.dot_general(
        slope_portion, gate_portion, (((0,), (0,)), ((), ())), preferred_element_type=jnp.float32
    )
    speed_deriv = jnp.sum(slope, axis=0)

    def flatten(member):
        return member.reshape(tokens, feature_span).astype(jnp.bfloat16)

    return (
        flatten(blended_response),
        flatten(acceptor_deriv),
        flatten(lookup_deriv),
        flatten(payload_deriv),
        input_gradient,
        (
            lowering_array_deriv,
            raising_array_deriv,
            speed_deriv,
            present_reward_deriv.reshape(feature_span),
        ),
    )


def shard_link(decays, own_states, pull_states):
    ahead_total, ahead = compose(decays, own_states, False)
    behind_total, behind = compose(decays, pull_states, True)
    identity = (jnp.ones_like(ahead_total[0]), jnp.zeros_like(ahead_total[1]))
    prior, state_in = entering_2(ahead_total, SEQ, follow, identity, False)
    latter, grad_after = entering_2(behind_total, SEQ, follow, identity, True)
    starts = ahead[0][..., None] * state_in[None] + ahead[1]
    block_ends = behind[0][..., None] * grad_after[None] + behind[1]
    return (starts, block_ends)


def per_device(
    acceptors,
    lookups,
    payloads,
    lagged_fading_source,
    response_cotangent,
    fading_lowering_array,
    fading_raising_array,
    feature_fading_speed,
    present_reward,
):
    collected_outcomes = sublevel_evaluation(
        acceptors[0],
        lookups[0],
        payloads[0],
        lagged_fading_source[0],
        response_cotangent[0],
        fading_lowering_array,
        fading_raising_array,
        feature_fading_speed,
        present_reward,
        shard_link,
    )
    sums = collected_outcomes[5]
    dp_count = lax.axis_size("dp")
    share_rows = fading_lowering_array.shape[0] // dp_count
    whole = lax.psum((sums[0], sums[1], sums[2], sums[3]), SEQ_DP)
    offset = lax.axis_index("dp") * share_rows
    reduced = tuple((lax.dynamic_slice_in_dim(member, offset, share_rows, 0) for member in whole))
    return (
        collected_outcomes[0][None],
        collected_outcomes[1][None],
        collected_outcomes[2][None],
        collected_outcomes[3][None],
        collected_outcomes[4][None],
        reduced[0],
        reduced[1],
        reduced[2],
        reduced[3],
    )


def solution(mesh):
    split = Mesh(
        mesh.devices.reshape(4, 2, 4, 2, mesh.shape["dp"]),
        ("seq_0", "seq_1", "seq_2", "seq_3", "dp"),
    )
    placed = (
        P("dp", SEQ, None),
        P("dp", SEQ, None),
        P("dp", SEQ, None),
        P("dp", SEQ, None),
        P("dp", SEQ, None),
        P(),
        P(),
        P(),
        P(),
    )
    return jax.shard_map(
        per_device,
        mesh=split,
        in_specs=placed,
        out_specs=(
            P("dp", SEQ, None),
            P("dp", SEQ, None),
            P("dp", SEQ, None),
            P("dp", SEQ, None),
            P("dp", SEQ, None),
            P("dp", None),
            P("dp", None),
            P("dp"),
            P("dp"),
        ),
        check_vma=False,
    )
```

profile of v0, /device:TPU:1, one launch (start us, length us, event | category | flops | bytes accessed | tf_op | source)
XLA Modules:
  0.0 685.3 jit_solution(13759978778250514535)
XLA Ops:
  28.3 7.0 %fusion.62 = f32[2,40,64,64]{2,3,1,0:T(8,128)} fusion(f32[2,64,40,64]{1,3,2,0:T(8,128)} %copy.91, bf16[2,64,40,64]{3,2,1,0:T(8,128)(2,1)} %reshape.319, f32[2,64,40,64]{1,3,2,0:T(8,128)S(1)} %copy.89, f32[2,64,40,64]{1,3,2,0:T(8,128)} %copy.90), kind=kOutput, calls=%fused_computation.117 | convolution fusion | flops 252313600 | bytes 5898240 | tf_op jit(solution)/shard_map/nchk,nchv->nhkv/dot_general | solution.py:39
  37.2 28.0 %while.39 = (s32[]{:T(128)}, f32[40,64]{1,0:T(8,128)S(1)}, f32[40,64,64]{2,1,0:T(8,128)}, f32[2,40,64]{2,1,0:T(8,128)S(1)}, f32[2,40,64,64]{2,3,1,0:T(8,128)}, /...) while((s32[]{:T(128)}, f32[40,64]{1,0:T(8,128)S(1)}, ...), condition=%wide.region_6.7_spmd.clone, body=%wide.region_5.6_spmd.clone.sunk | while | flops 499204 | bytes 9267333 | solution.py:72
  83.0 17.7 %while.38 = (s32[]{:T(128)}, f32[40,64]{1,0:T(8,128)S(1)}, f32[40,64,64]{2,1,0:T(8,128)}, f32[2,40,64]{2,1,0:T(8,128)S(1)}, f32[2,40,64,64]{2,3,1,0:T(8,128)}, /...) while((s32[]{:T(128)}, f32[40,64]{1,0:T(8,128)S(1)}, ...), condition=%wide.region_3.4_spmd.clone, body=%wide.region_2.3_spmd.clone.sunk | while | flops 499203 | bytes 6646389 | solution.py:72
  111.3 7.6 %all-gather.27.cloned.1.call-done = f32[80,64,64]{2,1,0:T(8,128)} async-done(((f32[40,64,64]{2,1,0:T(8,128)}), f32[80,64,64]{2,1,0:T(8,128)}) %all-gather.27.cloned.1.call-update) | async-done | bytes 1310736 | tf_op jit(solution)/shard_map/all_gather | solution.py:28
  122.1 9.9 %all-gather.5 = f32[160,64]{1,0:T(8,128)S(1)} all-gather(f32[40,64]{1,0:T(8,128)S(1)} %get-tuple-element.372), channel_id=7, replica_groups=mesh['seq_0'=4,'seq_1'=2,'seq_2'=4,'seq_3'=2,'dp'=2] {'seq_2'}, dimensions={0}, use_global_device_ids=true | all-gather | bytes 51200 | tf_op jit(solution)/shard_map/all_gather | solution.py:28
  138.8 39.7 %all-gather.21.cloned.1.call-done = f32[4,40,64,64]{3,2,1,0:T(8,128)} async-done(((f32[1,40,64,64]{3,2,1,0:T(8,128)}), f32[4,40,64,64]{3,2,1,0:T(8,128)}) %all-gather.21.cloned.1.call-update) | async-done | bytes 2621456 | tf_op jit(solution)/shard_map/all_gather | solution.py:28
  183.5 9.2 %all-gather.4 = f32[160,64]{1,0:T(8,128)S(1)} all-gather(f32[40,64]{1,0:T(8,128)} %get-tuple-element.377), channel_id=6, replica_groups=mesh['seq_0'=4,'seq_1'=2,'seq_2'=4,'seq_3'=2,'dp'=2] {'seq_2'}, dimensions={0}, use_global_device_ids=true | all-gather | bytes 51200 | tf_op jit(solution)/shard_map/all_gather | solution.py:28
  200.2 37.4 %all-gather.15.cloned.1.call-done = f32[4,40,64,64]{3,2,1,0:T(8,128)} async-done(((f32[1,40,64,64]{3,2,1,0:T(8,128)}), f32[4,40,64,64]{3,2,1,0:T(8,128)}) %all-gather.15.cloned.1.call-update) | async-done | bytes 2621456 | tf_op jit(solution)/shard_map/all_gather | solution.py:28
  243.8 38.6 %all-gather.23.cloned.1.call-done = f32[2,40,64,64]{3,2,1,0:T(8,128)} async-done(((f32[1,40,64,64]{3,2,1,0:T(8,128)}), f32[2,40,64,64]{3,2,1,0:T(8,128)}) %all-gather.23.cloned.1.call-update) | async-done | bytes 1310736 | tf_op jit(solution)/shard_map/all_gather | solution.py:28
  287.4 39.0 %all-gather.17.cloned.1.call-done = f32[2,40,64,64]{3,2,1,0:T(8,128)} async-done(((f32[1,40,64,64]{3,2,1,0:T(8,128)}), f32[2,40,64,64]{3,2,1,0:T(8,128)}) %all-gather.17.cloned.1.call-update) | async-done | bytes 1310736 | tf_op jit(solution)/shard_map/all_gather | solution.py:28
  339.8 11.4 %all_gather.86 = f32[4,40,64]{2,1,0:T(8,128)S(1)} all-gather(f32[1,40,64]{2,1,0:T(8,128)} %get-tuple-element.370), channel_id=1, replica_groups=mesh['seq_0'=4,'seq_1'=2,'seq_2'=4,'seq_3'=2,'dp'=2] {'seq_0'}, dimensions={0}, use_global_device_ids=true | all-gather | bytes 51200 | tf_op jit(solution)/shard_map/all_gather | solution.py:28
  351.2 11.1 %all_gather.76 = f32[4,40,64]{2,1,0:T(8,128)S(1)} all-gather(f32[1,40,64]{2,1,0:T(8,128)} %get-tuple-element.375), channel_id=1, replica_groups=mesh['seq_0'=4,'seq_1'=2,'seq_2'=4,'seq_3'=2,'dp'=2] {'seq_0'}, dimensions={0}, use_global_device_ids=true | all-gather | bytes 51200 | tf_op jit(solution)/shard_map/all_gather | solution.py:28
  370.5 8.1 %fusion.64 = f32[2,40,64,64]{3,2,1,0:T(8,128)} fusion(f32[2,64,40,64]{1,3,2,0:T(8,128)S(1)} %copy-done.3, f32[2,64,40,64]{1,3,2,0:T(8,128)S(1)} %copy.89, f32[2,40,64]{2,1,0:T(8,128)S(1)} %get-tuple-element.350, f32[2,64,40,64]{1,3,2,0:T(8,128)S(1)} %copy-done.6, f32[2,64,40,64]{1,3,2,0:T(8,128)S(1)} %copy-done.1), kind=kOutput, calls=%fused_computation.118 | convolution fusion | flops 253296640 | bytes 6574080 | tf_op jit(solution)/shard_map/nthk,nshk->nhts/dot_general | solution.py:39
  378.6 7.2 %all-gather.25.cloned.1.call-done = f32[4,40,64,64]{3,2,1,0:T(8,128)} async-done(((f32[1,40,64,64]{3,2,1,0:T(8,128)}), f32[4,40,64,64]{3,2,1,0:T(8,128)}) %all-gather.25.cloned.1.call-update) | async-done | bytes 2621456 | tf_op jit(solution)/shard_map/all_gather | solution.py:28
  385.8 9.0 %fusion.36 = f32[40,64,64]{2,1,0:T(8,128)} fusion(f32[4,40,64,64]{3,2,1,0:T(8,128)} %all-gather.25.cloned.1.call-done, f32[4,40,64,64]{3,2,1,0:T(8,128)} %all-gather.21.cloned.1.call-done, f32[2,40,64,64]{3,2,1,0:T(8,128)} %all-gather.23.cloned.1.call-done, f32[80,64,64]{2,1,0:T(8,128)} %all-gather.29.cloned.1.call-done, f32[40,64]{1,0:T(8,128)} %get-tuple-element.337, ...), kind=kLoop, calls=%fused_computation.65 | loop fusion | flops 6225920 | bytes 8673292 | tf_op jit(solution)/shard_map/mul | solution.py:229
  397.7 47.1 %all-gather.19.cloned.1.call-done = f32[4,40,64,64]{3,2,1,0:T(8,128)} async-done(((f32[1,40,64,64]{3,2,1,0:T(8,128)}), f32[4,40,64,64]{3,2,1,0:T(8,128)}) %all-gather.19.cloned.1.call-update) | async-done | bytes 2621456 | tf_op jit(solution)/shard_map/all_gather | solution.py:28
  444.8 9.0 %fusion.42 = f32[40,64,64]{2,1,0:T(8,128)} fusion(f32[4,40,64,64]{3,2,1,0:T(8,128)} %all-gather.19.cloned.1.call-done, f32[4,40,64,64]{3,2,1,0:T(8,128)} %all-gather.15.cloned.1.call-done, f32[2,40,64,64]{3,2,1,0:T(8,128)} %all-gather.17.cloned.1.call-done, f32[80,64,64]{2,1,0:T(8,128)} %all-gather.27.cloned.1.call-done, f32[40,64]{1,0:T(8,128)} %get-tuple-element.340, ...), kind=kLoop, calls=%fused_computation.83 | loop fusion | flops 6225920 | bytes 8673292 | tf_op jit(solution)/shard_map/mul | solution.py:228
  470.4 6.5 fusion.9
  476.9 11.0 %multiply_subtract_fusion = (f32[2,64,40,64]{1,3,2,0:T(8,128)}, f32[2,64,40,64]{1,3,2,0:T(8,128)}, bf16[2,64,40,64]{1,3,2,0:T(8,128)(2,1)}, bf16[2,64,40,64]{1,3,2,0:T(8,128)(2,1)}, f32[2,64,40]{1,2,0:T(8,128)}) fusion(f32[2,64,40,64]{1,3,2,0:T(8,128)S(1)} %copy-done.4, f32[2,64,40,64]{1,3,2,0:T(8,128)S(1)} %copy-done.7, f32[2,64,40,64]{1,3,2,0:T(8,128)} %fusion.9, ...), kind=kOutput, calls=%fused_computation.35 | convolution fusion | flops 258862080 | bytes 13203456 | tf_op jit(solution)/shard_map/nhst,nshk->nthk/dot_general | solution.py:39
  513.6 6.7 fusion.23
  522.5 7.2 %fusion.7 = bf16[2,64,40,64]{3,1,2,0:T(8,128)(2,1)} fusion(f32[2,40,64,64]{2,3,1,0:T(8,128)} %fusion.23, f32[2,40,64,64]{3,2,1,0:T(8,128)} %fusion.64, f32[2,64,40]{1,2,0:T(8,128)S(1)} %copy-done.28, pred[64,64]{1,0:T(8,128)(4,1)S(1)} %iota_compare_fusion, bf16[2,64,40,64]{3,2,1,0:T(8,128)(2,1)} %reshape.319), kind=kOutput, calls=%fused_computation.26 | convolution fusion | flops 253624320 | bytes 3956736 | tf_op jit(solution)/shard_map/nhst,nshv->nthv/dot_general | solution.py:39
  529.7 66.3 %all-reduce = (f32[2560]{0:T(1024)S(1)}, f32[2560]{0:T(1024)S(1)}) all-reduce(f32[2560]{0:T(1024)S(1)} %get-tuple-element.348, f32[2560]{0:T(1024)S(1)} %copy-done.40), channel_id=1, replica_groups=mesh['seq_0'=4,'seq_1'=2,'seq_2'=4,'seq_3'=2,'dp'=2] {'seq_0','seq_1','s..., use_global_device_ids=true, to_apply=%region_12.13 | all-reduce | flops 5120 | bytes 40960 | tf_op jit(solution)/shard_map/psum | solution.py:259
  603.4 8.8 %fusion.22 = f32[2,40,64,64]{2,3,1,0:T(8,128)S(1)} fusion(f32[2,40,64,64]{2,3,1,0:T(8,128)} %get-tuple-element.196, f32[40,64,64]{1,2,0:T(8,128)} %copy.103, f32[2,40,64]{2,1,0:T(8,128)S(1)} %get-tuple-element.193, f32[2,64,40,64]{1,3,2,0:T(8,128)} %copy.91, f32[2,64,40,64]{1,3,2,0:T(8,128)S(1)} %copy.89, f32[2,64,40,64]{1,3,2,0:T(8,128)} %copy.90), kind=kOutput, calls=%fused_computation.58 | convolution fusion | flops 252968960 | bytes 7229440 | tf_op jit(solution)/shard_map/nthk,nhkv->nthv/dot_general | solution.py:39
  623.5 51.8 %all-reduce.4.cloned.1.call-done = (f32[2560,128]{0,1:T(8,128)}, f32[2560,128]{1,0:T(8,128)}) async-done(((f32[2560,128]{0,1:T(8,128)}, f32[2560,128]{1,0:T(8,128)}), (f32[2560,128]{0,1:T(8,128)}, f32[2560,128]{1,0:T(8,128)})) %all-reduce.4.cloned.1.call-update) | async-done | bytes 2621456 | tf_op jit(solution)/shard_map/psum | solution.py:259
  (211 shorter events, 221.2 us)
Async XLA Ops:
  7.2 98.0 %all-gather.29.cloned.1.call-start = ((), (), s32[]{:S(2)}) async-start(), calls=%async_computation.7 | async-start | bytes 3932160 | tf_op jit(solution)/shard_map/all_gather | solution.py:28
  65.8 53.1 %all-gather.27.cloned.1.call-start = ((), (), s32[]{:S(2)}) async-start(), calls=%async_computation.6 | async-start | bytes 3932160 | tf_op jit(solution)/shard_map/all_gather | solution.py:28
  100.7 77.8 %all-gather.21.cloned.1.call-start = ((), (), s32[]{:S(2)}) async-start(), calls=%async_computation.3 | async-start | bytes 6553600 | tf_op jit(solution)/shard_map/all_gather | solution.py:28
  105.1 16.9 %copy-start.37 = (f32[40,64]{1,0:T(8,128)}, f32[40,64]{1,0:T(8,128)S(1)}, u32[]{:S(2)}) copy-start(f32[40,64]{1,0:T(8,128)S(1)} %get-tuple-element.372) | copy-start | bytes 30724
  108.2 129.4 %all-gather.15.cloned.1.call-start = ((), (), s32[]{:S(2)}) async-start(), calls=%async_computation | async-start | bytes 6553600 | tf_op jit(solution)/shard_map/all_gather | solution.py:28
  111.3 10.6 %copy-start.38 = (f32[40,64]{1,0:T(8,128)}, f32[40,64]{1,0:T(8,128)S(1)}, u32[]{:S(2)}) copy-start(f32[40,64]{1,0:T(8,128)S(1)} %get-tuple-element.378) | copy-start | bytes 30724
  122.0 160.4 %all-gather.23.cloned.1.call-start = ((), (), s32[]{:S(2)}) async-start(), calls=%async_computation.4 | async-start | bytes 3932160 | tf_op jit(solution)/shard_map/all_gather | solution.py:28
  183.4 143.0 %all-gather.17.cloned.1.call-start = ((), (), s32[]{:S(2)}) async-start(), calls=%async_computation.1 | async-start | bytes 3932160 | tf_op jit(solution)/shard_map/all_gather | solution.py:28
  242.6 143.2 %all-gather.25.cloned.1.call-start = ((), (), s32[]{:S(2)}) async-start(), calls=%async_computation.5 | async-start | bytes 6553600 | tf_op jit(solution)/shard_map/all_gather | solution.py:28
  285.4 159.3 %all-gather.19.cloned.1.call-start = ((), (), s32[]{:S(2)}) async-start(), calls=%async_computation.2 | async-start | bytes 6553600 | tf_op jit(solution)/shard_map/all_gather | solution.py:28
  329.5 345.8 %all-reduce.4.cloned.1.call-start = ((), (), s32[]{:S(2)}) async-start(), calls=%async_computation.8 | async-start | bytes 5242880 | tf_op jit(solution)/shard_map/psum | solution.py:259
  362.3 8.2 %copy-start.6 = (f32[2,64,40,64]{1,3,2,0:T(8,128)S(1)}, f32[2,64,40,64]{1,3,2,0:T(8,128)}, u32[]{:S(2)}) copy-start(f32[2,64,40,64]{1,3,2,0:T(8,128)} %copy.91) | copy-start | bytes 3932164
  370.5 15.3 %copy-start.32 = (f32[40,64]{1,0:T(8,128)S(1)}, f32[40,64]{1,0:T(8,128)}, u32[]{:S(2)}) copy-start(f32[40,64]{1,0:T(8,128)} %get-tuple-element.356) | copy-start | bytes 30724
  370.5 15.3 %copy-start.33 = (f32[40,64]{1,0:T(8,128)S(1)}, f32[40,64]{1,0:T(8,128)}, u32[]{:S(2)}) copy-start(f32[40,64]{1,0:T(8,128)} %get-tuple-element.357) | copy-start | bytes 30724
  394.8 50.0 %copy-start.34 = (f32[40,64]{1,0:T(8,128)S(1)}, f32[40,64]{1,0:T(8,128)}, u32[]{:S(2)}) copy-start(f32[40,64]{1,0:T(8,128)} %get-tuple-element.365) | copy-start | bytes 30724
  394.8 50.0 %copy-start.35 = (f32[40,64]{1,0:T(8,128)S(1)}, f32[40,64]{1,0:T(8,128)}, u32[]{:S(2)}) copy-start(f32[40,64]{1,0:T(8,128)} %get-tuple-element.366) | copy-start | bytes 30724
  456.6 6.4 copy-start.12
  470.4 6.5 copy-start.7
  470.4 6.5 copy-start.27
  470.4 6.5 copy-start.36
  513.6 6.7 copy-start.20
  522.5 7.2 %copy-start.40 = (f32[2560]{0:T(1024)S(1)}, f32[2560]{0:T(1024)}, u32[]{:S(2)}) copy-start(f32[2560]{0:T(1024)} %multiply_reduce_fusion.2) | copy-start | bytes 30724
  603.4 8.8 %copy-start.10 = (bf16[2,64,40,64]{3,2,1,0:T(8,128)(2,1)S(1)}, bf16[2,64,40,64]{3,2,1,0:T(8,128)(2,1)}, u32[]{:S(2)}) copy-start(bf16[2,64,40,64]{3,2,1,0:T(8,128)(2,1)} %reshape.318) | copy-start | bytes 1966084
  603.4 8.8 %copy-start.14 = (f32[2,40,64,64]{3,2,1,0:T(8,128)S(1)}, f32[2,40,64,64]{3,2,1,0:T(8,128)}, u32[]{:S(2)}) copy-start(f32[2,40,64,64]{3,2,1,0:T(8,128)} %fusion.64) | copy-start | bytes 3932164
  (27 other events, 71.6 us)
Sparse Core Ops, SparseCore 0:
  65.4 17.6 all-gather.28
  100.8 18.0 all-gather.26
  120.6 57.8 all-gather.20
  180.0 57.5 all-gather.14
  239.1 43.2 all-gather.22
  283.9 42.4 all-gather.16
  328.1 57.6 all-gather.24
  387.5 57.2 all-gather.18
  521.9 153.3 all-reduce.3
where the time goes:
time: 694 us; the launch traced here: 685 us
  waiting for transfers between devices  268 us (39%)
  blocking collectives  123 us (18%)
  local copies, waits for them, and re-layouts  111 us (16%)
  other arithmetic  84.8 us (12%)
  matrix products  83.6 us (12%)
  between operations  14.6 us (2%)
    all_gather x8, waiting for transfers between devices, entering_2(): pieces = jax.tree.map(lambda part: lax.all_gather(part, axis), subtotal)  216 us
    dot_general x12, matrix products, contract(): jnp.einsum(pattern, left, right, precision=HIGH, preferred_element_type=j...  76.2 us
    psum x1, blocking collectives, per_device(): whole = lax.psum((sums[0], sums[1], sums[2], sums[3]), SEQ_DP)  66.3 us
    all_gather x8, blocking collectives, entering_2(): pieces = jax.tree.map(lambda part: lax.all_gather(part, axis), subtotal)  56.3 us
    psum x1, waiting for transfers between devices, per_device(): whole = lax.psum((sums[0], sums[1], sums[2], sums[3]), SEQ_DP)  51.8 us
    add x6, other arithmetic, follow(): return (earlier[0] * later[0], later[0][..., None] * earlier[1] + later[1])  22 us
    dynamic_update_slice x8, local copies, waits for them, and re-layouts, compose(): return lax.scan(advance, initial, (decays, own_states), reverse=backward)  21.3 us
  transfers between devices with their start and end apart: 9, of which 8 were waited for; matrix products, arithmetic and copies ran while one was open for 20% of the time, Pallas kernels for 0%

commit v1 on v0

v1 whole, which is shorter than its diff:
```python
import functools

import jax
import jax.numpy as jnp
from jax import lax
from jax.experimental import pallas as pl
from jax.experimental.pallas import tpu as pltpu
from jax.sharding import PartitionSpec as P

F32 = jnp.float32
BF16 = jnp.bfloat16
TOK = 128
HALF = 64
GROUPS = 4
PAIRS = 5
WIDTH = PAIRS * 128
CHIPS = 32
NN = (((1,), (0,)), ((), ()))
NT = (((1,), (1,)), ((), ()))
TN = (((0,), (0,)), ((), ()))


def dot(a, b, dims):
    return lax.dot_general(a, b, dims, preferred_element_type=F32)


def split(x, parts):
    pieces = []
    for _ in range(parts - 1):
        head = x.astype(BF16)
        pieces.append(head)
        x = x - head.astype(F32)
    pieces.append(x.astype(BF16))
    return pieces


def summed_by(matrix, x, parts):
    total = None
    for piece in split(x, parts):
        term = dot(matrix, piece, NN)
        total = term if total is None else total + term
    return total


def grids():
    row = lax.broadcasted_iota(jnp.int32, (TOK, TOK), 0)
    col = lax.broadcasted_iota(jnp.int32, (TOK, TOK), 1)
    same = (row < HALF) == (col < HALF)
    return row, col, same


def as_matrix(condition):
    return jnp.where(condition, 1.0, 0.0).astype(BF16)


def decay_sums(gate, raising, speed, lower):
    rank = dot(gate, raising, NT)
    log_decay = -speed * jnp.exp(rank)
    inclusive = summed_by(lower, log_decay, 3)
    return (
        log_decay,
        inclusive,
        inclusive - log_decay,
        inclusive[HALF - 1 : HALF],
        inclusive[TOK - 1 : TOK],
    )


def packed(product, left):
    return jnp.where(left[:HALF], product[:HALF], product[HALF:])


def spread(state, left):
    low = state.astype(BF16)
    zero = jnp.zeros_like(low)
    return jnp.concatenate(
        [jnp.where(left[:HALF], low, zero), jnp.where(left[:HALF], zero, low)], axis=0
    )


def first_kernel(
    x_ref, a_ref, r_ref, k_ref, v_ref, g_ref, b_ref, speed_ref,
    state_ref, decay_ref, smooth_ref, gate_ref,
):
    @pl.when(pl.program_id(0) == 0)
    def _():
        smooth = jnp.tanh(dot(x_ref[...], a_ref[...], NN))
        smooth_ref[...] = smooth
        gate_ref[...] = smooth.astype(BF16)

    row, col, same = grids()
    lower = as_matrix(same & (row >= col))
    left = col < HALF
    early = row < HALF
    gate = gate_ref[...]
    for pair in range(PAIRS):
        at = pl.ds(pair * 128, 128)
        _, inclusive, exclusive, total0, total1 = decay_sums(
            gate, b_ref[at, :], speed_ref[:, at], lower
        )
        to_end = jnp.exp(jnp.where(early, total0 + total1, total1) - inclusive)
        from_start = jnp.exp(jnp.where(early, exclusive, exclusive + total0))
        keys = (k_ref[:, at].astype(F32) * to_end).astype(BF16)
        reads = (r_ref[:, at].astype(F32) * from_start).astype(BF16)
        own = packed(dot(v_ref[:, at], keys, TN), left)
        pull = packed(dot(g_ref[:, at], reads, TN), left)
        rows = slice(pair * 8, pair * 8 + 8)
        state_ref[0, :, rows, :] = own.reshape(8, 8, 128)
        state_ref[1, :, rows, :] = pull.reshape(8, 8, 128)
        decay_ref[0, pair : pair + 1, :] = jnp.exp(total0 + total1)
    decay_ref[0, PAIRS:, :] = jnp.zeros((8 - PAIRS, 128), F32)


def first_stage(x, a, r, k, v, g, b, speed):
    tokens = pl.BlockSpec((TOK, WIDTH), lambda i: (0, i))
    whole = lambda shape: pl.BlockSpec(shape, lambda i: (0,) * len(shape))
    channels = x.shape[1]
    return pl.pallas_call(
        first_kernel,
        grid=(GROUPS,),
        in_specs=[
            whole((TOK, channels)),
            whole((channels, 128)),
            tokens,
            tokens,
            tokens,
            tokens,
            pl.BlockSpec((WIDTH, 128), lambda i: (i, 0)),
            pl.BlockSpec((1, WIDTH), lambda i: (0, i)),
        ],
        out_specs=[
            pl.BlockSpec((2, 8, 40, 128), lambda i: (0, i, 0, 0)),
            pl.BlockSpec((1, 8, 128), lambda i: (i, 0, 0)),
            whole((TOK, 128)),
            whole((TOK, 128)),
        ],
        out_shape=[
            jax.ShapeDtypeStruct((2, 32, 40, 128), F32),
            jax.ShapeDtypeStruct((GROUPS, 8, 128), F32),
            jax.ShapeDtypeStruct((TOK, 128), F32),
            jax.ShapeDtypeStruct((TOK, 128), BF16),
        ],
        name="first_stage",
    )(x, a, r, k, v, g, b, speed)


def second_kernel(
    x_ref, a_ref, r_ref, k_ref, v_ref, g_ref, b_ref, speed_ref, reward_ref,
    smooth_ref, gate_ref, state_ref,
    mixed_ref, dr_ref, dk_ref, dv_ref, dx_ref, sums_ref,
    slope_ref, acc_ref,
):
    group = pl.program_id(0)
    row, col, same = grids()
    lower = as_matrix(same & (row >= col))
    ones = as_matrix((row < HALF) == (col < HALF))
    left = col < HALF
    early = row < HALF
    wide_row = lax.broadcasted_iota(jnp.int32, (TOK, 2 * TOK), 0)
    wide_col = lax.broadcasted_iota(jnp.int32, (TOK, 2 * TOK), 1) % TOK
    wide_same = (wide_row < HALF) == (wide_col < HALF)
    beneath = wide_same & (wide_row > wide_col)
    above = wide_same & (wide_row < wide_col)
    around = jnp.where(
        same & ~early & (col < row), 1.0, jnp.where(same & early & (col >= row), -1.0, 0.0)
    ).astype(BF16)

    @pl.when(group == 0)
    def _():
        acc_ref[...] = jnp.zeros_like(acc_ref)
        sums_ref[:, :, 40:, :] = jnp.zeros((2, 64, 8, 128), F32)

    gate = gate_ref[...]

    def by_head(x):
        zero = jnp.zeros_like(x)
        return jnp.concatenate([jnp.where(left, x, zero), jnp.where(left, zero, x)], axis=0)

    for pair in range(PAIRS):
        at = pl.ds(pair * 128, 128)
        log_decay, inclusive, exclusive, total0, total1 = decay_sums(
            gate, b_ref[at, :], speed_ref[:, at], lower
        )
        middle = jnp.where(
            early, inclusive[HALF // 2 - 1 : HALF // 2], inclusive[HALF + HALF // 2 - 1 : HALF + HALF // 2]
        )
        entering = jnp.exp(exclusive)
        leaving = jnp.exp(jnp.where(early, total0, total1) - inclusive)
        upward = jnp.exp(exclusive - middle)
        downward = jnp.exp(middle - inclusive)
        r16, k16, v16, g16 = r_ref[:, at], k_ref[:, at], v_ref[:, at], g_ref[:, at]
        r, k, v, g = (t.astype(F32) for t in (r16, k16, v16, g16))
        reward = reward_ref[:, at]
        reached = (r * entering).astype(BF16)
        faded = (k * leaving).astype(BF16)
        up = (r * upward).astype(BF16)
        down = (k * downward).astype(BF16)
        v2, g2, up2, down2 = by_head(v16), by_head(g16), by_head(up), by_head(down)

        rows = slice(pair * 8, pair * 8 + 8)
        start0 = state_ref[0, :, rows, :].reshape(HALF, 128)
        end1 = state_ref[1, :, rows, :].reshape(HALF, 128)
        own0 = packed(dot(v16[:HALF], faded[:HALF], TN), left)
        pull1 = packed(dot(g16[HALF:], reached[HALF:], TN), left)
        start1 = jnp.exp(total0) * start0 + own0
        end0 = jnp.exp(total1) * end1 + pull1
        coupling = jnp.where(
            early,
            jnp.sum(end0.astype(BF16).astype(F32) * start1, axis=0, keepdims=True),
            jnp.sum(end0 * start1.astype(BF16).astype(F32), axis=0, keepdims=True),
        )
        s0, s1, e0, e1 = (spread(t, left) for t in (start0, start1, end0, end1))

        def both(lhs, first, last, dims):
            return jnp.concatenate(
                [dot(lhs[:HALF], first, dims), dot(lhs[HALF:], last, dims)], axis=0
            )

        zero = jnp.zeros((), F32)
        scores = jnp.where(beneath, dot(up, down2, NT), zero).astype(BF16)
        scores_t = jnp.where(above, dot(down, up2, NT), zero).astype(BF16)
        products = jnp.where(beneath, dot(g16, v2, NT), zero).astype(BF16)
        products_t = jnp.where(above, dot(v16, g2, NT), zero).astype(BF16)

        present = None
        for piece in split(r * reward * k, 2):
            term = dot(piece, ones, NN)
            present = term if present is None else present + term
        agreement = None
        for piece in split(v * g, 2):
            term = dot(piece, ones, NN)
            agreement = term if agreement is None else agreement + term

        mixed_ref[:, at] = (
            dot(scores, v2, NN) + present * v + both(reached, s0, s1, NT)
        ).astype(BF16)
        dv_ref[:, at] = (
            both(faded, e0, e1, NT) + dot(scores_t, g2, NN) + present * g
        ).astype(BF16)
        past = both(g16, s0, s1, NN)
        near_past = dot(products, down2, NN)
        later = both(v16, e0, e1, NN)
        near_later = dot(products_t, up2, NN)
        dr_ref[:, at] = (
            entering * past + upward * near_past + reward * k * agreement
        ).astype(BF16)
        dk_ref[:, at] = (
            leaving * later + downward * near_later + reward * r * agreement
        ).astype(BF16)
        read = reached.astype(F32) * past + up.astype(F32) * near_past
        change = faded.astype(F32) * later + down.astype(F32) * near_later - read
        slope = (coupling + summed_by(around, change, 2) - read) * log_decay
        slope16 = slope.astype(BF16)
        slope_ref[:, at] = slope16
        chunk = 32 * (group // 2) + PAIRS * (group % 2) + pair
        sums_ref[0, chunk, 40:41, :] = jnp.sum(slope, axis=0, keepdims=True)
        sums_ref[1, chunk, 40:41, :] = jnp.sum(r * k * agreement, axis=0, keepdims=True)

    slopes = slope_ref[...]
    acc_ref[...] += dot(slopes, b_ref[...], NN)
    sums_ref[1, pl.ds(group * 16, 16), :40, :] = dot(slopes, gate, TN).reshape(16, 40, 128)

    @pl.when(group == GROUPS - 1)
    def _():
        smooth = smooth_ref[...]
        project = (acc_ref[...] * (1.0 - smooth * smooth)).astype(BF16)
        for i in range(GROUPS):
            at = pl.ds(i * WIDTH, WIDTH)
            dx_ref[:, at] = dot(project, a_ref[at, :], NT).astype(BF16)
            sums_ref[0, i * 16 : i * 16 + 16, :40, :] = dot(x_ref[:, at], project, TN).reshape(
                16, 40, 128
            )


def second_stage(x, a, r, k, v, g, b, speed, reward, smooth, gate, states):
    tokens = pl.BlockSpec((TOK, WIDTH), lambda i: (0, i))
    whole = lambda shape: pl.BlockSpec(shape, lambda i: (0,) * len(shape))
    channels = x.shape[1]
    full = jax.ShapeDtypeStruct((TOK, channels), BF16)
    return pl.pallas_call(
        second_kernel,
        grid=(GROUPS,),
        in_specs=[
            whole((TOK, channels)),
            whole((channels, 128)),
            tokens,
            tokens,
            tokens,
            tokens,
            pl.BlockSpec((WIDTH, 128), lambda i: (i, 0)),
            pl.BlockSpec((1, WIDTH), lambda i: (0, i)),
            pl.BlockSpec((1, WIDTH), lambda i: (0, i)),
            whole((TOK, 128)),
            whole((TOK, 128)),
            pl.BlockSpec((2, 8, 40, 128), lambda i: (0, i, 0, 0)),
        ],
        out_specs=[
            tokens,
            tokens,
            tokens,
            tokens,
            whole((TOK, channels)),
            whole((2, 64, 48, 128)),
        ],
        out_shape=[full] * 5 + [jax.ShapeDtypeStruct((2, 64, 48, 128), F32)],
        scratch_shapes=[pltpu.VMEM((TOK, WIDTH), BF16), pltpu.VMEM((TOK, 128), F32)],
        name="second_stage",
    )(x, a, r, k, v, g, b, speed, reward, smooth, gate, states)


def place():
    seq = lax.axis_index("seq")
    return seq // 2, seq % 2


def scan_kernel(
    z_ref, d_ref, o_ref,
    x_ref, dx_ref, dc_ref, t_ref, r_ref, q_ref, p_ref, y_ref,
    swap_send, swap_recv, out_send, out_recv, back_send, back_recv, end_send, end_recv,
):
    chip, core = place()
    other = 1 - core
    partner = {"seq": chip * 2 + other}

    def peer(m):
        return {"seq": m * 2 + core}

    def turn(o):
        return lax.rem(chip + o, CHIPS)

    barrier = pltpu.get_barrier_semaphore()
    pl.semaphore_signal(barrier, inc=1, device_id=partner)

    @pl.loop(1, CHIPS)
    def _(o):
        pl.semaphore_signal(barrier, inc=1, device_id=peer(turn(o)))

    pl.semaphore_wait(barrier, CHIPS)

    swap = pltpu.make_async_remote_copy(
        z_ref.at[other], x_ref, swap_send.at[0], swap_recv.at[0], device_id=partner
    )
    swap_decay = pltpu.make_async_remote_copy(
        d_ref, dx_ref, swap_send.at[1], swap_recv.at[1], device_id=partner
    )
    swap_decay.start()
    swap.start()
    swap_decay.wait_recv()
    dc_ref[...] = d_ref[...] * dx_ref[...]
    swap.wait_recv()

    def out_copy(m, slot):
        return pltpu.make_async_remote_copy(
            t_ref.at[m], r_ref.at[slot], out_send.at[m], out_recv.at[slot], device_id=peer(m)
        )

    def back_copy(n, slot):
        return pltpu.make_async_remote_copy(
            q_ref.at[n], p_ref.at[slot], back_send.at[n], back_recv.at[slot], device_id=peer(n)
        )

    def end_copy(m):
        return pltpu.make_async_remote_copy(
            y_ref.at[m], o_ref.at[core, m], end_send.at[m], end_recv.at[m], device_id=partner
        )

    def end_wait(m):
        pltpu.make_async_remote_copy(
            y_ref.at[m], o_ref.at[other, m], end_send.at[m], end_recv.at[m], device_id=partner
        ).wait_recv()

    def chip_total(m, target):
        group = m // 8
        for j in range(PAIRS):
            rows = slice(8 * j, 8 * j + 8)
            target[rows, :] = dx_ref[group, j : j + 1, :] * z_ref[core, m, rows, :] + x_ref[m, rows, :]
        target[40:48, :] = dc_ref[group]

    chip_total(chip, r_ref.at[chip])

    @pl.loop(1, CHIPS)
    def _(o):
        m = turn(o)
        chip_total(m, t_ref.at[m])
        out_copy(m, chip).start()

    def step(i, carry):
        n = core * (CHIPS - 1) + (1 - 2 * core) * i

        @pl.when(n != chip)
        def _():
            out_copy(n, n).wait_recv()

        after = []
        for j in range(PAIRS):
            rows = slice(8 * j, 8 * j + 8)
            q_ref[n, rows, :] = carry[j]
            after.append(r_ref[n, 40 + j : 41 + j, :] * carry[j] + r_ref[n, rows, :])

        @pl.when(n != chip)
        def _():
            back_copy(n, chip).start()

        return tuple(after)

    lax.fori_loop(0, CHIPS, step, tuple(jnp.zeros((8, 128), F32) for _ in range(PAIRS)))

    def finish(m, source):
        group = m // 8
        o_ref[core, m] = source[...]
        for j in range(PAIRS):
            rows = slice(8 * j, 8 * j + 8)
            y_ref[m, rows, :] = d_ref[group, j : j + 1, :] * source[rows, :] + z_ref[core, m, rows, :]
        end_copy(m).start()

    finish(chip, q_ref.at[chip])

    @pl.loop(1, CHIPS)
    def _(o):
        m = turn(o)
        back_copy(m, m).wait_recv()
        finish(m, p_ref.at[m])

    end_wait(chip)
    swap.wait_send()
    swap_decay.wait_send()
    end_copy(chip).wait_send()

    @pl.loop(1, CHIPS)
    def _(o):
        m = turn(o)
        end_wait(m)
        out_copy(m, chip).wait_send()
        back_copy(m, chip).wait_send()
        end_copy(m).wait_send()


def scan_stage(states, decays):
    vmem = pl.BlockSpec(memory_space=pltpu.VMEM)
    state = pltpu.VMEM((32, 40, 128), F32)
    message = pltpu.VMEM((32, 48, 128), F32)
    decay = pltpu.VMEM((GROUPS, 8, 128), F32)
    sems = pltpu.SemaphoreType.DMA
    return pl.pallas_call(
        scan_kernel,
        in_specs=[vmem, vmem],
        out_specs=vmem,
        out_shape=jax.ShapeDtypeStruct((2, 32, 40, 128), F32),
        scratch_shapes=[state, decay, decay, message, message, state, state, state]
        + [sems((2,)), sems((2,))]
        + [sems((CHIPS,))] * 6,
        compiler_params=pltpu.CompilerParams(collective_id=0, has_side_effects=True),
        name="scan_stage",
    )(states, decays)


def reduce_stage(sums):
    whole = lax.psum(sums, ("seq", "dp"))
    return lax.dynamic_slice_in_dim(whole, lax.axis_index("dp") * 32, 32, 1)


def per_device(scan, reduce, r, k, v, x, g, lowering, raising, speed, reward):
    r, k, v, x, g = (t[0] for t in (r, k, v, x, g))
    speed, reward = speed[None], reward[None]
    states, decays, smooth, gate = first_stage(x, lowering, r, k, v, g, raising, speed)
    entering = scan(states, decays)
    mixed, dr, dk, dv, dx, sums = second_stage(
        x, lowering, r, k, v, g, raising, speed, reward, smooth, gate, entering
    )
    share = reduce(sums)
    return (
        mixed[None],
        dr[None],
        dk[None],
        dv[None],
        dx[None],
        share[0, :, :40].reshape(1280, 128),
        share[1, :, :40].reshape(1280, 128),
        share[0, :10, 40].reshape(1280),
        share[1, :10, 40].reshape(1280),
    )


def build(mesh, scan, reduce):
    tokens = P("dp", "seq", None)
    return jax.shard_map(
        functools.partial(per_device, scan, reduce),
        mesh=mesh,
        in_specs=(tokens,) * 5 + (P(),) * 4,
        out_specs=(tokens,) * 5 + (P("dp", None),) * 2 + (P("dp"),) * 2,
        check_vma=False,
    )


def solution(mesh):
    return build(mesh, scan_stage, reduce_stage)
```

time: 694 us -> 242 us (0.35); the launches traced: 685 us -> 242 us
  blocking collectives: 123 us -> 0 us
  waiting for transfers between devices: 268 us -> 152 us
  local copies, waits for them, and re-layouts: 111 us -> 6.47 us
  other arithmetic: 84.8 us -> 0 us
  matrix products: 83.6 us -> 0 us
  Pallas kernels: 0 us -> 69.7 us
    all_gather x8 -> x0, waiting for transfers between devices: 216 us -> none  [entering_2(): pieces = jax.tree.map(lambda part: lax.all_gather(part, axis), subtotal)]
    psum x1, waiting for transfers between devices: 51.8 us -> 152 us  [reduce_stage(): whole = lax.psum(sums, ('seq', 'dp'))]
    dot_general x18 -> x0, matrix products: 83.6 us -> none  [the longest x12 76.2 us: contract(): jnp.einsum(pattern, left, right, precision=HIGH, preferred_element_type=j...]
    pallas_call x0 -> x3, Pallas kernels: none -> 69.7 us  [the longest x1 40.4 us: scan_stage(): pl.pallas_call(scan_kernel, in_specs=[vmem, vmem], out_specs=vmem, out_sh...]
    psum x1 -> x0, blocking collectives: 66.3 us -> none  [per_device(): whole = lax.psum((sums[0], sums[1], sums[2], sums[3]), SEQ_DP)]
    all_gather x8 -> x0, blocking collectives: 56.3 us -> none  [entering_2(): pieces = jax.tree.map(lambda part: lax.all_gather(part, axis), subtotal)]
    mul x18 -> x0, other arithmetic: 27.1 us -> none  [the longest x1 9.03 us: shard_link(): starts = ahead[0][..., None] * state_in[None] + ahead[1]]
    convert_element_type x12 -> x0, local copies, waits for them, and re-layouts: 26 us -> none  [the longest x8 13.8 us: flatten(): return member.reshape(tokens, feature_span).astype(jnp.bfloat16)]
  transfers between devices with their start and end apart: 9 -> 1, of which waited for: 8 -> 1; matrix products, arithmetic and copies ran while one was open for 20% -> 0% of each run, Pallas kernels for 0% -> 0%
where the time goes in v1:
time: 242 us
  waiting for transfers between devices  152 us (63%)
  Pallas kernels  69.7 us (29%)
  between operations  14.1 us (6%)
  local copies, waits for them, and re-layouts  6.47 us (3%)
    psum x1, waiting for transfers between devices, reduce_stage(): whole = lax.psum(sums, ('seq', 'dp'))  152 us
    pallas_call x1, Pallas kernels, scan_stage(): pl.pallas_call(scan_kernel, in_specs=[vmem, vmem], out_specs=vmem, out_sh...  40.4 us
    pallas_call x1, Pallas kernels, second_stage(): pl.pallas_call(second_kernel, grid=(GROUPS,), in_specs=[whole((TOK, chann...  20.6 us
    pallas_call x1, Pallas kernels, first_stage(): pl.pallas_call(first_kernel, grid=(GROUPS,), in_specs=[whole((TOK, channe...  8.76 us
  transfers between devices with their start and end apart: 1, of which 1 were waited for; matrix products, arithmetic and copies ran while one was open for 0% of the time, Pallas kernels for 0%

profile of v1, /device:TPU:1, one launch (start us, length us, event | category | flops | bytes accessed | tf_op | source)
XLA Modules:
  0.0 242.1 jit_solution(13639952569937861727)
XLA Ops:
  7.2 0.0 all-reduce.2.cloned.1.call-start
  7.2 1.3 broadcast_in_dim.21.speed_ref
  8.5 1.3 broadcast_in_dim.22.reward_ref
  9.8 8.8 %first_stage.1 = (f32[2,32,40,128]{3,2,1,0:T(8,128)}, f32[4,8,128]{2,1,0:T(8,128)}, f32[128,128]{1,0:T(8,128)}, bf16[128,128]{1,0:T(8,128)(2,1)}) custom-call(bf16[128,2560]{1,0:T(8,128)(2,1)} %bitcast.14, bf16[2560,128]{1,0:T(8,128)(2,1)} %a_ref.3, bf16[128,2560]{1,0:T(8,128)(2,1)} %bitcast.16, bf16[128,2560]{1,0:T(8,128)(2,1)} %bitcast.18, ...), custom_call_target="tpu_custom_call" | custom-call | tf_op jit(solution)/shard_map/first_stage/pallas_call | solution.py:118
  18.6 40.4 %scan_stage.1.state_ref = f32[2,32,40,128]{3,2,1,0:T(8,128)} custom-call(f32[2,32,40,128]{3,2,1,0:T(8,128)} %get-tuple-element.21.z_ref, f32[4,8,128]{2,1,0:T(8,128)} %get-tuple-element.22.d_ref), custom_call_target="tpu_custom_call" | custom-call | tf_op jit(solution)/shard_map/scan_stage/pallas_call | solution.py:444
  59.0 20.6 %second_stage.1 = (bf16[128,2560]{1,0:T(8,128)(2,1)}, bf16[128,2560]{1,0:T(8,128)(2,1)}, bf16[128,2560]{1,0:T(8,128)(2,1)}, bf16[128,2560]{1,0:T(8,128)(2,1)}, b...) custom-call(bf16[128,2560]{1,0:T(8,128)(2,1)} %bitcast.15, bf16[2560,128]{1,0:T(8,128)(2,1)} %a_ref.3, ...), custom_call_target="tpu_custom_call" | custom-call | tf_op jit(solution)/shard_map/second_stage/pallas_call | solution.py:280
  79.6 0.0 all-reduce.2.cloned.1.call-update
  79.6 151.7 %all-reduce.2.cloned.1.call-done = f32[2,64,48,128]{3,2,1,0:T(8,128)} async-done(((f32[2,64,48,128]{3,2,1,0:T(8,128)}), f32[2,64,48,128]{3,2,1,0:T(8,128)}) %all-reduce.2.cloned.1.call-update) | async-done | bytes 3145744 | tf_op jit(solution)/shard_map/psum | solution.py:458
  231.4 2.4 %constant_dynamic-slice_fusion = (f32[1,32,40,128]{3,2,1,0:T(8,128)}, f32[1,32,40,128]{3,2,1,0:T(8,128)}) fusion(f32[2,64,48,128]{3,2,1,0:T(8,128)} %all-reduce.2.cloned.1.call-done, s32[]{:T(128)S(6)} %add.8, s32[]{:T(128)S(6)} %select_n.3), kind=kLoop, calls=%fused_computation.2 | loop fusion | bytes 2621448 | tf_op jit(solution)/shard_map/slice | solution.py:478
  233.8 1.4 dynamic-slice_reduce_fusion
Async XLA Ops:
  7.2 224.2 %all-reduce.2.cloned.1.call-start = ((), (), s32[]{:S(2)}) async-start(), calls=%async_computation | async-start | bytes 6291456 | tf_op jit(solution)/shard_map/psum | solution.py:458
Sparse Core Ops, SparseCore 0:
  79.7 151.5 all-reduce.1

commit v2 on v1

--- a/solution.py
+++ b/solution.py
@@ -15,6 +15,9 @@
 PAIRS = 5
 WIDTH = PAIRS * 128
 CHIPS = 32
+CHUNKS = 2 * CHIPS
+PARTS = 8
+PART = CHUNKS // PARTS
 NN = (((1,), (0,)), ((), ()))
 NT = (((1,), (1,)), ((), ()))
 TN = (((0,), (0,)), ((), ()))
@@ -454,9 +457,136 @@
     )(states, decays)
 
 
+def reduce_kernel(
+    w_ref, o_ref,
+    x_ref, t_ref, r_ref, s_ref,
+    swap_send, swap_recv, out_send, out_recv, back_send, back_recv, end_send, end_recv,
+):
+    chip, core = place()
+    half = lax.axis_index("dp")
+    other = 1 - core
+    mine = half * CHIPS + chip
+    partner = {"seq": chip * 2 + other}
+
+    def peer(c):
+        return {"seq": lax.rem(c, CHIPS) * 2 + core, "dp": c // CHIPS}
+
+    def turn(o):
+        return lax.rem(mine + o, CHUNKS)
+
+    def near(o):
+        return lax.rem(chip + o, CHIPS)
+
+    barrier = pltpu.get_barrier_semaphore()
+    pl.semaphore_signal(barrier, inc=1, device_id=partner)
+
+    @pl.loop(1, CHUNKS)
+    def _(o):
+        pl.semaphore_signal(barrier, inc=1, device_id=peer(turn(o)))
+
+    pl.semaphore_wait(barrier, CHUNKS)
+
+    def swap_copy(part):
+        at = pl.ds(part * PART, PART)
+        return pltpu.make_async_remote_copy(
+            w_ref.at[other, at], x_ref.at[at], swap_send.at[part], swap_recv.at[part], device_id=partner
+        )
+
+    def out_copy(c, slot):
+        return pltpu.make_async_remote_copy(
+            t_ref.at[c], r_ref.at[slot], out_send.at[c], out_recv.at[slot], device_id=peer(c)
+        )
+
+    def back_copy(n):
+        return pltpu.make_async_remote_copy(
+            s_ref, o_ref.at[core, chip], back_send.at[n], back_recv.at[chip],
+            device_id={"seq": n * 2 + core},
+        )
+
+    def back_wait(n):
+        pltpu.make_async_remote_copy(
+            s_ref, o_ref.at[core, n], back_send.at[n], back_recv.at[n],
+            device_id={"seq": n * 2 + core},
+        ).wait_recv()
+
+    def end_copy(n):
+        return pltpu.make_async_remote_copy(
+            o_ref.at[core, n], o_ref.at[core, n], end_send.at[n], end_recv.at[n], device_id=partner
+        )
+
+    def end_wait(n):
+        pltpu.make_async_remote_copy(
+            o_ref.at[other, n], o_ref.at[other, n], end_send.at[n], end_recv.at[n], device_id=partner
+        ).wait_recv()
+
+    for part in range(PARTS):
+        swap_copy(part).start()
+    for part in range(PARTS):
+        swap_copy(part).wait_recv()
+
+        @pl.loop(part * PART, part * PART + PART)
+        def _(c):
+            t_ref[c] = w_ref[core, c] + x_ref[c]
+
+            @pl.when(c != mine)
+            def _():
+                out_copy(c, mine).start()
+
+    def add(o, total):
+        c = turn(o)
+        out_copy(c, c).wait_recv()
+        return total + r_ref[c]
+
+    s_ref[...] = lax.fori_loop(1, CHUNKS, add, t_ref[mine])
+
+    @pl.loop(1, CHIPS)
+    def _(o):
+        back_copy(near(o)).start()
+
+    o_ref[core, chip] = s_ref[...]
+    end_copy(chip).start()
+
+    @pl.loop(1, CHIPS)
+    def _(o):
+        n = near(o)
+        back_wait(n)
+        end_copy(n).start()
+
+    for part in range(PARTS):
+        swap_copy(part).wait_send()
+
+    @pl.loop(1, CHUNKS)
+    def _(o):
+        out_copy(turn(o), mine).wait_send()
+
+    @pl.loop(0, CHIPS)
+    def _(o):
+        n = near(o)
+        end_wait(n)
+        end_copy(n).wait_send()
+
+    @pl.loop(1, CHIPS)
+    def _(o):
+        back_copy(near(o)).wait_send()
+
+
 def reduce_stage(sums):
-    whole = lax.psum(sums, ("seq", "dp"))
-    return lax.dynamic_slice_in_dim(whole, lax.axis_index("dp") * 32, 32, 1)
+    vmem = pl.BlockSpec(memory_space=pltpu.VMEM)
+    rows = sums.shape[2]
+    chunks = pltpu.VMEM((CHUNKS, rows, 128), F32)
+    sems = pltpu.SemaphoreType.DMA
+    return pl.pallas_call(
+        reduce_kernel,
+        in_specs=[vmem],
+        out_specs=vmem,
+        out_shape=jax.ShapeDtypeStruct((2, CHIPS, rows, 128), F32),
+        scratch_shapes=[chunks, chunks, chunks, pltpu.VMEM((rows, 128), F32)]
+        + [sems((PARTS,))] * 2
+        + [sems((CHUNKS,))] * 2
+        + [sems((CHIPS,))] * 4,
+        compiler_params=pltpu.CompilerParams(collective_id=1, has_side_effects=True),
+        name="reduce_stage",
+    )(sums)
 
 
 def per_device(scan, reduce, r, k, v, x, g, lowering, raising, speed, reward):

time: 242 us -> 138 us (0.57)
  the two profiles are of different devices: /device:TPU:1 before, /device:TPU:23 now
where the time goes in v2:
time: 138 us
  Pallas kernels  131 us (95%)
  local copies, waits for them, and re-layouts  6.47 us (5%)
    pallas_call x1, Pallas kernels, reduce_stage(): pl.pallas_call(reduce_kernel, in_specs=[vmem], out_specs=vmem, out_shape=...  64.3 us
    pallas_call x1, Pallas kernels, scan_stage(): pl.pallas_call(scan_kernel, in_specs=[vmem, vmem], out_specs=vmem, out_sh...  37.1 us
    pallas_call x1, Pallas kernels, second_stage(): pl.pallas_call(second_kernel, grid=(GROUPS,), in_specs=[whole((TOK, chann...  20.6 us
    pallas_call x1, Pallas kernels, first_stage(): pl.pallas_call(first_kernel, grid=(GROUPS,), in_specs=[whole((TOK, channe...  8.76 us

profile of v2, /device:TPU:23, one launch (start us, length us, event | category | flops | bytes accessed | tf_op | source)
XLA Modules:
  0.0 137.9 jit_solution(16999464289893257345)
XLA Ops:
  0.6 1.3 broadcast_in_dim.21.speed_ref
  1.9 1.3 broadcast_in_dim.22.reward_ref
  3.3 8.8 %first_stage.1 = (f32[2,32,40,128]{3,2,1,0:T(8,128)}, f32[4,8,128]{2,1,0:T(8,128)}, f32[128,128]{1,0:T(8,128)}, bf16[128,128]{1,0:T(8,128)(2,1)}) custom-call(bf16[128,2560]{1,0:T(8,128)(2,1)} %bitcast.14, bf16[2560,128]{1,0:T(8,128)(2,1)} %a_ref.3, bf16[128,2560]{1,0:T(8,128)(2,1)} %bitcast.16, bf16[128,2560]{1,0:T(8,128)(2,1)} %bitcast.18, ...), custom_call_target="tpu_custom_call" | custom-call | tf_op jit(solution)/shard_map/first_stage/pallas_call | solution.py:121
  12.0 37.1 %scan_stage.1.state_ref = f32[2,32,40,128]{3,2,1,0:T(8,128)} custom-call(f32[2,32,40,128]{3,2,1,0:T(8,128)} %get-tuple-element.21.z_ref, f32[4,8,128]{2,1,0:T(8,128)} %get-tuple-element.22.d_ref), custom_call_target="tpu_custom_call" | custom-call | tf_op jit(solution)/shard_map/scan_stage/pallas_call | solution.py:447
  49.1 20.6 %second_stage.1 = (bf16[128,2560]{1,0:T(8,128)(2,1)}, bf16[128,2560]{1,0:T(8,128)(2,1)}, bf16[128,2560]{1,0:T(8,128)(2,1)}, bf16[128,2560]{1,0:T(8,128)(2,1)}, b...) custom-call(bf16[128,2560]{1,0:T(8,128)(2,1)} %bitcast.15, bf16[2560,128]{1,0:T(8,128)(2,1)} %a_ref.3, ...), custom_call_target="tpu_custom_call" | custom-call | tf_op jit(solution)/shard_map/second_stage/pallas_call | solution.py:283
  69.7 64.3 %reduce_stage.1 = f32[2,32,48,128]{3,2,1,0:T(8,128)} custom-call(f32[2,64,48,128]{3,2,1,0:T(8,128)} %get-tuple-element.28.w_ref), custom_call_target="tpu_custom_call" | custom-call | tf_op jit(solution)/shard_map/reduce_stage/pallas_call | solution.py:578
  134.0 1.4 %slice_reduce_fusion = (f32[10,128]{1,0:T(8,128)}, f32[10,128]{1,0:T(8,128)}) fusion(f32[2,32,48,128]{3,2,1,0:T(8,128)} %reduce_stage.1), kind=kLoop, calls=%fused_computation | loop fusion | bytes 20480 | tf_op jit(solution)/shard_map/slice | solution.py:610
  135.4 2.4 %fusion = (f32[1,32,40,128]{3,2,1,0:T(8,128)}, f32[1,32,40,128]{3,2,1,0:T(8,128)}) fusion(f32[2,32,48,128]{3,2,1,0:T(8,128)} %reduce_stage.1), kind=kLoop, calls=%fused_computation.2 | loop fusion | bytes 2621440 | tf_op jit(solution)/shard_map/slice | solution.py:608
